TPU v7x, 32 devices: a whole 2x2x4 slice. The times are simulated.
32 devices in a mesh: row: 8 (over z, y), col: 4 (over x, core).
Axes of the slice: x: 2, y: 2, z: 4, core: 2. Of those that a mesh axis runs over, the one named last changes fastest.
Arguments:
- hidden_act: bfloat16 [768, 26624], P('col', 'row'), may hold values from -6 to 6
- out_grad: bfloat16 [768, 16384], P('row', 'col'), may hold values from -6 to 6
- down_weight: bfloat16 [26624, 16384], P('row', 'col'), may hold values from -0.046875 to 0.046875
Outputs:
- fisher: float32 [26624, 16384], P('row', 'col')
- hidden_grad: bfloat16 [768, 26624], P('col', 'row')
All inputs are finite; a program needn't handle non-finite values.
Results may differ from a plain program's by a relative error of at most 0.001.
Values may be sent and summed in bfloat16 or wider, within the bound.
No kernel may reach another device: no remote copies, remote signals or barrier semaphores. Data moves between devices by JAX's collectives and lax.ppermute only.
A program may use at most 192 MiB of HBM per device.

v0:
```python
import jax
import jax.numpy as jnp
from jax import lax
from jax.sharding import PartitionSpec as P

SEQ = 96
EXAMPLES = 8


def per_device(hidden_act, out_grad, down_weight):
    act_whole = lax.all_gather(hidden_act, "col", axis=0, tiled=True)
    grad_whole = lax.all_gather(out_grad, "row", axis=0, tiled=True)
    feat_rows = down_weight.shape[0]
    feat_cols = down_weight.shape[1]

    def accumulate(example, total):
        start = (example * SEQ).astype(jnp.int32)
        act_piece = lax.dynamic_slice_in_dim(act_whole, start, SEQ, 0)
        grad_piece = lax.dynamic_slice_in_dim(grad_whole, start, SEQ, 0)
        grad_e = lax.dot_general(
            act_piece, grad_piece, (((0,), (0,)), ((), ())), preferred_element_type=jnp.float32
        )
        return total + grad_e * grad_e

    total = lax.fori_loop(0, EXAMPLES, accumulate, jnp.zeros((feat_rows, feat_cols), jnp.float32))
    fisher = total / (EXAMPLES * SEQ)
    summed = lax.psum_scatter(
        lax.dot_general(
            grad_whole, down_weight, (((1,), (1,)), ((), ())), preferred_element_type=jnp.float32
        ),
        "col",
        scatter_dimension=0,
        tiled=True,
    )
    return (fisher, summed.astype(jnp.bfloat16))


def solution(mesh):
    placed = (P("col", "row"), P("row", "col"), P("row", "col"))
    return jax.shard_map(
        per_device,
        mesh=mesh,
        in_specs=placed,
        out_specs=(P("row", "col"), P("col", "row")),
        check_vma=False,
    )
```

profile of v0, /device:TPU:0, one launch (start us, length us, event | category | flops | bytes accessed | tf_op | source)
XLA Modules:
  0.0 478.3 jit_solution(6444310962151930377)
XLA Ops:
  7.2 0.0 all-gather.5.cloned.1.call-start
  7.2 0.7 all-gather.5.cloned.1.call-update
  7.9 0.0 all-gather.3.cloned.1.call-start
  7.9 0.7 all-gather.3.cloned.1.call-update
  8.6 0.0 reduce-scatter.2.cloned.1.call-start
  8.7 102.9 %all-gather.5.cloned.1.call-done = bf16[768,4096]{1,0:T(8,128)(2,1)} async-done(((bf16[96,4096]{1,0:T(8,128)(2,1)}), bf16[768,4096]{1,0:T(8,128)(2,1)}) %all-gather.5.cloned.1.call-update) | async-done | bytes 6291472 | tf_op jit(solution)/shard_map/all_gather | solution.py:12
  111.6 29.3 %fusion.3 = f32[768,3328]{1,0:T(8,128)} fusion(bf16[768,4096]{1,0:T(8,128)(2,1)} %all-gather.5.cloned.1.call-done, bf16[3328,4096]{1,0:T(8,128)(2,1)} %param.7), kind=kOutput, calls=%fused_computation.5 | convolution fusion | flops 20937965568 | bytes 43778048 | tf_op jit(solution)/shard_map/dot_general | solution.py:28
  140.9 0.0 reduce-scatter.2.cloned.1.call-update
  140.9 10.1 %all-gather.3.cloned.1.call-done = bf16[768,3328]{1,0:T(8,128)(2,1)} async-done(((bf16[192,3328]{1,0:T(8,128)(2,1)}), bf16[768,3328]{1,0:T(8,128)(2,1)}) %all-gather.3.cloned.1.call-update) | async-done | bytes 5111824 | tf_op jit(solution)/shard_map/all_gather | solution.py:11
  151.0 282.1 %while.14 = (s32[]{:T(128)}, f32[3328,4096]{1,0:T(8,128)}, bf16[768,3328]{1,0:T(8,128)(2,1)}, bf16[768,4096]{1,0:T(8,128)(2,1)}, s32[]{:T(128)}, /*index=5*/s32[]{:T(128)}, s32[]{:T(128)}, s32[]{:T(128)}) while((s32[]{:T(128)}, f32[3328,4096]{1,0:T(8,128)}, bf16[768,3328]{1,0:T(8,128)(2,1)}, bf16[768,4096]{1,0:T(8,128)(2,1)}, ...), condition=%wide.region_1.0_spmd.clone, body=%wide.region_0.0_spmd.clone.sunk | while | flops 2658140160 | bytes 110478984 | solution.py:25
  151.0 25.6 %select_add_fusion.2 = f32[3328,4096]{1,0:T(8,128)} fusion(f32[3328,4096]{1,0:T(8,128)} %get-tuple-element.139, pred[]{:T(512)S(6)} %compare.3, bf16[768,4096]{1,0:T(8,128)(2,1)} %get-tuple-element.149, s32[]{:T(128)S(6)} %select_n.10, bf16[768,3328]{1,0:T(8,128)(2,1)} %get-tuple-element.148), kind=kOutput, calls=%fused_computation.clone.1 | convolution fusion | flops 2658140160 | bytes 110478848 | tf_op jit(solution)/shard_map/while/body/eval_jaxpr/dot_general | solution.py:20
  176.7 38.3 %select_add_fusion.2 = f32[3328,4096]{1,0:T(8,128)} fusion(f32[3328,4096]{1,0:T(8,128)} %get-tuple-element.139, pred[]{:T(512)S(6)} %compare.3, bf16[768,4096]{1,0:T(8,128)(2,1)} %get-tuple-element.149, s32[]{:T(128)S(6)} %select_n.10, bf16[768,3328]{1,0:T(8,128)(2,1)} %get-tuple-element.148), kind=kOutput, calls=%fused_computation.clone.1 | convolution fusion | flops 2658140160 | bytes 110478848 | tf_op jit(solution)/shard_map/while/body/eval_jaxpr/dot_general | solution.py:20
  215.0 36.6 %select_add_fusion.2 = f32[3328,4096]{1,0:T(8,128)} fusion(f32[3328,4096]{1,0:T(8,128)} %get-tuple-element.139, pred[]{:T(512)S(6)} %compare.3, bf16[768,4096]{1,0:T(8,128)(2,1)} %get-tuple-element.149, s32[]{:T(128)S(6)} %select_n.10, bf16[768,3328]{1,0:T(8,128)(2,1)} %get-tuple-element.148), kind=kOutput, calls=%fused_computation.clone.1 | convolution fusion | flops 2658140160 | bytes 110478848 | tf_op jit(solution)/shard_map/while/body/eval_jaxpr/dot_general | solution.py:20
  251.6 36.3 %select_add_fusion.2 = f32[3328,4096]{1,0:T(8,128)} fusion(f32[3328,4096]{1,0:T(8,128)} %get-tuple-element.139, pred[]{:T(512)S(6)} %compare.3, bf16[768,4096]{1,0:T(8,128)(2,1)} %get-tuple-element.149, s32[]{:T(128)S(6)} %select_n.10, bf16[768,3328]{1,0:T(8,128)(2,1)} %get-tuple-element.148), kind=kOutput, calls=%fused_computation.clone.1 | convolution fusion | flops 2658140160 | bytes 110478848 | tf_op jit(solution)/shard_map/while/body/eval_jaxpr/dot_general | solution.py:20
  287.9 36.3 %select_add_fusion.2 = f32[3328,4096]{1,0:T(8,128)} fusion(f32[3328,4096]{1,0:T(8,128)} %get-tuple-element.139, pred[]{:T(512)S(6)} %compare.3, bf16[768,4096]{1,0:T(8,128)(2,1)} %get-tuple-element.149, s32[]{:T(128)S(6)} %select_n.10, bf16[768,3328]{1,0:T(8,128)(2,1)} %get-tuple-element.148), kind=kOutput, calls=%fused_computation.clone.1 | convolution fusion | flops 2658140160 | bytes 110478848 | tf_op jit(solution)/shard_map/while/body/eval_jaxpr/dot_general | solution.py:20
  324.2 36.3 %select_add_fusion.2 = f32[3328,4096]{1,0:T(8,128)} fusion(f32[3328,4096]{1,0:T(8,128)} %get-tuple-element.139, pred[]{:T(512)S(6)} %compare.3, bf16[768,4096]{1,0:T(8,128)(2,1)} %get-tuple-element.149, s32[]{:T(128)S(6)} %select_n.10, bf16[768,3328]{1,0:T(8,128)(2,1)} %get-tuple-element.148), kind=kOutput, calls=%fused_computation.clone.1 | convolution fusion | flops 2658140160 | bytes 110478848 | tf_op jit(solution)/shard_map/while/body/eval_jaxpr/dot_general | solution.py:20
  360.5 36.3 %select_add_fusion.2 = f32[3328,4096]{1,0:T(8,128)} fusion(f32[3328,4096]{1,0:T(8,128)} %get-tuple-element.139, pred[]{:T(512)S(6)} %compare.3, bf16[768,4096]{1,0:T(8,128)(2,1)} %get-tuple-element.149, s32[]{:T(128)S(6)} %select_n.10, bf16[768,3328]{1,0:T(8,128)(2,1)} %get-tuple-element.148), kind=kOutput, calls=%fused_computation.clone.1 | convolution fusion | flops 2658140160 | bytes 110478848 | tf_op jit(solution)/shard_map/while/body/eval_jaxpr/dot_general | solution.py:20
  396.8 36.3 %select_add_fusion.2 = f32[3328,4096]{1,0:T(8,128)} fusion(f32[3328,4096]{1,0:T(8,128)} %get-tuple-element.139, pred[]{:T(512)S(6)} %compare.3, bf16[768,4096]{1,0:T(8,128)(2,1)} %get-tuple-element.149, s32[]{:T(128)S(6)} %select_n.10, bf16[768,3328]{1,0:T(8,128)(2,1)} %get-tuple-element.148), kind=kOutput, calls=%fused_computation.clone.1 | convolution fusion | flops 2658140160 | bytes 110478848 | tf_op jit(solution)/shard_map/while/body/eval_jaxpr/dot_general | solution.py:20
  433.1 35.8 %broadcast_multiply_fusion = f32[3328,4096]{1,0:T(8,128)} fusion(f32[3328,4096]{1,0:T(8,128)} %get-tuple-element.81), kind=kLoop, calls=%fused_computation.4 | loop fusion | flops 13631488 | bytes 109051904 | tf_op jit(solution)/shard_map/div | solution.py:26
  468.9 0.0 reduce-scatter.2.cloned.1.call-done
  468.9 2.9 convert_element_type.3
  (1 shorter events, 0.0 us)
Async XLA Ops:
  7.2 104.4 %all-gather.5.cloned.1.call-start = ((), (), s32[]{:S(2)}) async-start(), calls=%async_computation.2 | async-start | bytes 7077888 | tf_op jit(solution)/shard_map/all_gather | solution.py:12
  7.9 143.1 %all-gather.3.cloned.1.call-start = ((), (), s32[]{:S(2)}) async-start(), calls=%async_computation.1 | async-start | bytes 6389760 | tf_op jit(solution)/shard_map/all_gather | solution.py:11
  8.6 460.2 %reduce-scatter.2.cloned.1.call-start = ((), (), s32[]{:S(2)}) async-start(), calls=%async_computation.3 | async-start | bytes 12779520 | tf_op jit(solution)/shard_map/reduce_scatter | solution.py:27
Sparse Core Ops, SparseCore 0:
  10.2 101.4 all-gather.4
  113.2 37.8 all-gather.2
  153.7 82.7 reduce-scatter.1
where the time goes:
time: 478 us
  matrix products  311 us (65%)
  waiting for transfers between devices  114 us (24%)
  other arithmetic  38.7 us (8%)
  between operations  13.8 us (3%)
    dot_general x8, matrix products, accumulate(): lax.dot_general(act_piece, grad_piece, (((0,), (0,)), ((), ())), preferre...  282 us
    all_gather x1, waiting for transfers between devices, per_device(): grad_whole = lax.all_gather(out_grad, 'row', axis=0, tiled=True)  103 us
    div x1, other arithmetic, per_device(): fisher = total / (EXAMPLES * SEQ)  35.8 us
    dot_general x1, matrix products, per_device(): lax.dot_general(grad_whole, down_weight, (((1,), (1,)), ((), ())), prefer...  29.3 us
    all_gather x1, waiting for transfers between devices, per_device(): act_whole = lax.all_gather(hidden_act, 'col', axis=0, tiled=True)  10.1 us
  transfers between devices with their start and end apart: 3, of which 2 were waited for; matrix products, arithmetic and copies ran while one was open for 73% of the time, Pallas kernels for 0%

commit v1 on v0

--- a/solution.py
+++ b/solution.py
@@ -9,7 +9,14 @@
 
 def per_device(hidden_act, out_grad, down_weight):
     act_whole = lax.all_gather(hidden_act, "col", axis=0, tiled=True)
-    grad_whole = lax.all_gather(out_grad, "row", axis=0, tiled=True)
+    ways = lax.axis_size("row")
+    pieces = [out_grad]
+    for far in range(1, ways):
+        pieces.append(
+            lax.ppermute(pieces[far - 1], "row", [(d, (d - 1) % ways) for d in range(ways)])
+        )
+    line = jnp.concatenate(pieces, axis=0)
+    grad_whole = jnp.roll(line, lax.axis_index("row") * out_grad.shape[0], axis=0)
     feat_rows = down_weight.shape[0]
     feat_cols = down_weight.shape[1]
 

time: 478 us -> 518 us (1.084)
  starting transfers between devices: 0.11 us -> 37.1 us
  local copies, waits for them, and re-layouts: 0 us -> 25.9 us
  waiting for transfers between devices: 114 us -> 91.3 us
    all_gather x1 -> x0, waiting for transfers between devices: 103 us -> none  [per_device(): grad_whole = lax.all_gather(out_grad, 'row', axis=0, tiled=True)]
    ppermute x0 -> x7, waiting for transfers between devices: none -> 91.2 us  [per_device(): lax.ppermute(pieces[far - 1], 'row', [(d, (d - 1) % ways) for d in range(...]
    ppermute x0 -> x7, starting transfers between devices: none -> 37.1 us  [per_device(): lax.ppermute(pieces[far - 1], 'row', [(d, (d - 1) % ways) for d in range(...]
    unnamed x0 -> x19, local copies, waits for them, and re-layouts: none -> 20.3 us
    all_gather x1, waiting for transfers between devices: 10.1 us -> 0.02 us  [per_device(): act_whole = lax.all_gather(hidden_act, 'col', axis=0, tiled=True)]
  transfers between devices with their start and end apart: 3 -> 9, of which waited for: 2 -> 7; matrix products, arithmetic and copies ran while one was open for 73% -> 71% of each run, Pallas kernels for 0% -> 0%
where the time goes in v1:
time: 518 us
  matrix products  311 us (60%)
  waiting for transfers between devices  91.3 us (18%)
  other arithmetic  38.7 us (7%)
  starting transfers between devices  37.1 us (7%)
  local copies, waits for them, and re-layouts  25.9 us (5%)
  between operations  14.1 us (3%)
    dot_general x8, matrix products, accumulate(): lax.dot_general(act_piece, grad_piece, (((0,), (0,)), ((), ())), preferre...  282 us
    ppermute x7, waiting for transfers between devices, per_device(): lax.ppermute(pieces[far - 1], 'row', [(d, (d - 1) % ways) for d in range(...  91.2 us
    ppermute x7, starting transfers between devices, per_device(): lax.ppermute(pieces[far - 1], 'row', [(d, (d - 1) % ways) for d in range(...  37.1 us
    div x1, other arithmetic, per_device(): fisher = total / (EXAMPLES * SEQ)  35.8 us
    dot_general x1, matrix products, per_device(): lax.dot_general(grad_whole, down_weight, (((1,), (1,)), ((), ())), prefer...  28.6 us
    unnamed x19, local copies, waits for them, and re-layouts  20.3 us
  transfers between devices with their start and end apart: 9, of which 7 were waited for; matrix products, arithmetic and copies ran while one was open for 71% of the time, Pallas kernels for 0%

profile of v1, /device:TPU:0, one launch (start us, length us, event | category | flops | bytes accessed | tf_op | source)
XLA Modules:
  0.0 518.1 jit_solution(691983155803898275)
XLA Ops:
  7.2 0.0 all-gather.2.cloned.1.call-start
  7.2 6.1 %collective-permute-start = (bf16[96,4096]{1,0:T(8,128)(2,1)}, bf16[96,4096]{1,0:T(8,128)(2,1)S(1)}, u32[]{:S(2)}, u32[]{:S(2)}) collective-permute-start(bf16[96,4096]{1,0:T(8,128)(2,1)} %param.6), channel_id=1, source_target_pairs={{0,28},{4,0},{8,4},{12,8},{16,12},{20,16},{24,20},{28,24},{1,29},{... | collective-permute-start | bytes 2359304 | tf_op jit(solution)/shard_map/ppermute | solution.py:16
  13.3 17.1 %collective-permute-done = bf16[96,4096]{1,0:T(8,128)(2,1)S(1)} collective-permute-done((bf16[96,4096]{1,0:T(8,128)(2,1)}, bf16[96,4096]{1,0:T(8,128)(2,1)S(1)}, u32[]{:S(2)}, u32[]{:S(2)}) %collective-permute-start) | collective-permute-done | bytes 786464 | tf_op jit(solution)/shard_map/ppermute | solution.py:16
  30.4 5.1 collective-permute-start.1
  35.5 15.9 %collective-permute-done.1 = bf16[96,4096]{1,0:T(8,128)(2,1)S(1)} collective-permute-done((bf16[96,4096]{1,0:T(8,128)(2,1)S(1)}, bf16[96,4096]{1,0:T(8,128)(2,1)S(1)}, u32[]{:S(2)}, u32[]{:S(2)}) %collective-permute-start.1) | collective-permute-done | bytes 786464 | tf_op jit(solution)/shard_map/ppermute | solution.py:16
  51.4 5.2 collective-permute-start.2
  56.6 15.1 %collective-permute-done.2 = bf16[96,4096]{1,0:T(8,128)(2,1)S(1)} collective-permute-done((bf16[96,4096]{1,0:T(8,128)(2,1)S(1)}, bf16[96,4096]{1,0:T(8,128)(2,1)S(1)}, u32[]{:S(2)}, u32[]{:S(2)}) %collective-permute-start.2) | collective-permute-done | bytes 786464 | tf_op jit(solution)/shard_map/ppermute | solution.py:16
  71.7 5.2 collective-permute-start.3
  76.9 0.0 all-gather.2.cloned.1.call-update
  76.9 0.0 reduce-scatter.2.cloned.1.call-start
  77.0 2.1 constant_dynamic-update-slice_fusion.15
  79.1 12.0 %collective-permute-done.3 = bf16[96,4096]{1,0:T(8,128)(2,1)} collective-permute-done((bf16[96,4096]{1,0:T(8,128)(2,1)S(1)}, bf16[96,4096]{1,0:T(8,128)(2,1)}, u32[]{:S(2)}, u32[]{:S(2)}) %collective-permute-start.3) | collective-permute-done | bytes 786464 | tf_op jit(solution)/shard_map/ppermute | solution.py:16
  91.1 5.3 %collective-permute-start.4 = (bf16[96,4096]{1,0:T(8,128)(2,1)}, bf16[96,4096]{1,0:T(8,128)(2,1)S(1)}, u32[]{:S(2)}, u32[]{:S(2)}) collective-permute-start(bf16[96,4096]{1,0:T(8,128)(2,1)} %collective-permute-done.3), channel_id=1, source_target_pairs={{0,28},{4,0},{8,4},{12,8},{16,12},{20,16},{24,20},{28,24},{1,29},{... | collective-permute-start | bytes 2359304 | tf_op jit(solution)/shard_map/ppermute | solution.py:16
  96.4 1.0 constant_dynamic-update-slice_fusion.14
  97.4 0.9 constant_dynamic-update-slice_fusion.13
  98.3 11.8 %collective-permute-done.4 = bf16[96,4096]{1,0:T(8,128)(2,1)S(1)} collective-permute-done((bf16[96,4096]{1,0:T(8,128)(2,1)}, bf16[96,4096]{1,0:T(8,128)(2,1)S(1)}, u32[]{:S(2)}, u32[]{:S(2)}) %collective-permute-start.4) | collective-permute-done | bytes 786464 | tf_op jit(solution)/shard_map/ppermute | solution.py:16
  110.1 5.1 collective-permute-start.5
  115.2 0.9 constant_dynamic-update-slice_fusion.12
  116.1 2.1 constant_dynamic-update-slice_fusion.11
  118.2 9.5 %collective-permute-done.5 = bf16[96,4096]{1,0:T(8,128)(2,1)S(1)} collective-permute-done((bf16[96,4096]{1,0:T(8,128)(2,1)S(1)}, bf16[96,4096]{1,0:T(8,128)(2,1)S(1)}, u32[]{:S(2)}, u32[]{:S(2)}) %collective-permute-start.5) | collective-permute-done | bytes 786464 | tf_op jit(solution)/shard_map/ppermute | solution.py:16
  127.7 5.2 %collective-permute-start.6 = (bf16[96,4096]{1,0:T(8,128)(2,1)S(1)}, bf16[96,4096]{1,0:T(8,128)(2,1)S(1)}, u32[]{:S(2)}, u32[]{:S(2)}) collective-permute-start(bf16[96,4096]{1,0:T(8,128)(2,1)S(1)} %collective-permute-done.5), channel_id=1, source_target_pairs={{0,28},{4,0},{8,4},{12,8},{16,12},{20,16},{24,20},{28,24},{1,29},{... | collective-permute-start | bytes 2359304 | tf_op jit(solution)/shard_map/ppermute | solution.py:16
  132.9 0.9 constant_dynamic-update-slice_fusion.10
  133.8 1.0 constant_dynamic-update-slice_fusion.9
  134.8 9.8 %collective-permute-done.6 = bf16[96,4096]{1,0:T(8,128)(2,1)S(1)} collective-permute-done((bf16[96,4096]{1,0:T(8,128)(2,1)S(1)}, bf16[96,4096]{1,0:T(8,128)(2,1)S(1)}, u32[]{:S(2)}, u32[]{:S(2)}) %collective-permute-start.6) | collective-permute-done | bytes 786464 | tf_op jit(solution)/shard_map/ppermute | solution.py:16
  144.5 0.9 constant_dynamic-update-slice_fusion.8
  145.5 1.0 constant_dynamic-update-slice_fusion.7
  146.4 0.9 constant_dynamic-update-slice_fusion.6
  147.4 1.0 constant_dynamic-update-slice_fusion.5
  148.4 1.0 constant_dynamic-update-slice_fusion.4
  149.4 2.1 constant_dynamic-update-slice_fusion.3
  151.5 0.9 constant_dynamic-update-slice_fusion.2
  152.5 0.9 constant_dynamic-update-slice_fusion.1
  153.4 1.0 constant_dynamic-update-slice_fusion
  154.3 4.6 constant_dynamic-slice_fusion
  159.0 2.6 copy-done
  161.6 28.6 %fusion.3 = f32[768,3328]{1,0:T(8,128)} fusion(bf16[768,4096]{1,0:T(8,128)(2,1)S(1)} %constant_dynamic-slice_fusion, bf16[3328,4096]{1,0:T(8,128)(2,1)} %param.7), kind=kOutput, calls=%fused_computation.22 | convolution fusion | flops 20937965568 | bytes 43778048 | tf_op jit(solution)/shard_map/dot_general | solution.py:35
  190.2 0.0 all-gather.2.cloned.1.call-done
  190.3 282.4 %while.14 = (s32[]{:T(128)}, f32[3328,4096]{1,0:T(8,128)}, bf16[768,3328]{1,0:T(8,128)(2,1)}, bf16[768,4096]{1,0:T(8,128)(2,1)}, s32[]{:T(128)}, /*index=5*/s32[]{:T(128)}, s32[]{:T(128)}, s32[]{:T(128)}) while((s32[]{:T(128)}, f32[3328,4096]{1,0:T(8,128)}, bf16[768,3328]{1,0:T(8,128)(2,1)}, bf16[768,4096]{1,0:T(8,128)(2,1)}, ...), condition=%wide.region_1.2_spmd.clone, body=%wide.region_0.1_spmd.clone.sunk | while | flops 2658140160 | bytes 110478984 | solution.py:32
  190.3 26.2 %select_add_fusion.2 = f32[3328,4096]{1,0:T(8,128)} fusion(f32[3328,4096]{1,0:T(8,128)} %get-tuple-element.139, pred[]{:T(512)S(6)} %compare.3, bf16[768,4096]{1,0:T(8,128)(2,1)} %get-tuple-element.149, s32[]{:T(128)S(6)} %select_n.25, bf16[768,3328]{1,0:T(8,128)(2,1)} %get-tuple-element.148), kind=kOutput, calls=%fused_computation.clone.1 | convolution fusion | flops 2658140160 | bytes 110478848 | tf_op jit(solution)/shard_map/while/body/eval_jaxpr/dot_general | solution.py:27
  216.4 38.2 %select_add_fusion.2 = f32[3328,4096]{1,0:T(8,128)} fusion(f32[3328,4096]{1,0:T(8,128)} %get-tuple-element.139, pred[]{:T(512)S(6)} %compare.3, bf16[768,4096]{1,0:T(8,128)(2,1)} %get-tuple-element.149, s32[]{:T(128)S(6)} %select_n.25, bf16[768,3328]{1,0:T(8,128)(2,1)} %get-tuple-element.148), kind=kOutput, calls=%fused_computation.clone.1 | convolution fusion | flops 2658140160 | bytes 110478848 | tf_op jit(solution)/shard_map/while/body/eval_jaxpr/dot_general | solution.py:27
  254.6 36.6 %select_add_fusion.2 = f32[3328,4096]{1,0:T(8,128)} fusion(f32[3328,4096]{1,0:T(8,128)} %get-tuple-element.139, pred[]{:T(512)S(6)} %compare.3, bf16[768,4096]{1,0:T(8,128)(2,1)} %get-tuple-element.149, s32[]{:T(128)S(6)} %select_n.25, bf16[768,3328]{1,0:T(8,128)(2,1)} %get-tuple-element.148), kind=kOutput, calls=%fused_computation.clone.1 | convolution fusion | flops 2658140160 | bytes 110478848 | tf_op jit(solution)/shard_map/while/body/eval_jaxpr/dot_general | solution.py:27
  291.2 36.3 %select_add_fusion.2 = f32[3328,4096]{1,0:T(8,128)} fusion(f32[3328,4096]{1,0:T(8,128)} %get-tuple-element.139, pred[]{:T(512)S(6)} %compare.3, bf16[768,4096]{1,0:T(8,128)(2,1)} %get-tuple-element.149, s32[]{:T(128)S(6)} %select_n.25, bf16[768,3328]{1,0:T(8,128)(2,1)} %get-tuple-element.148), kind=kOutput, calls=%fused_computation.clone.1 | convolution fusion | flops 2658140160 | bytes 110478848 | tf_op jit(solution)/shard_map/while/body/eval_jaxpr/dot_general | solution.py:27
  327.5 36.3 %select_add_fusion.2 = f32[3328,4096]{1,0:T(8,128)} fusion(f32[3328,4096]{1,0:T(8,128)} %get-tuple-element.139, pred[]{:T(512)S(6)} %compare.3, bf16[768,4096]{1,0:T(8,128)(2,1)} %get-tuple-element.149, s32[]{:T(128)S(6)} %select_n.25, bf16[768,3328]{1,0:T(8,128)(2,1)} %get-tuple-element.148), kind=kOutput, calls=%fused_computation.clone.1 | convolution fusion | flops 2658140160 | bytes 110478848 | tf_op jit(solution)/shard_map/while/body/eval_jaxpr/dot_general | solution.py:27
  363.8 36.3 %select_add_fusion.2 = f32[3328,4096]{1,0:T(8,128)} fusion(f32[3328,4096]{1,0:T(8,128)} %get-tuple-element.139, pred[]{:T(512)S(6)} %compare.3, bf16[768,4096]{1,0:T(8,128)(2,1)} %get-tuple-element.149, s32[]{:T(128)S(6)} %select_n.25, bf16[768,3328]{1,0:T(8,128)(2,1)} %get-tuple-element.148), kind=kOutput, calls=%fused_computation.clone.1 | convolution fusion | flops 2658140160 | bytes 110478848 | tf_op jit(solution)/shard_map/while/body/eval_jaxpr/dot_general | solution.py:27
  400.1 36.3 %select_add_fusion.2 = f32[3328,4096]{1,0:T(8,128)} fusion(f32[3328,4096]{1,0:T(8,128)} %get-tuple-element.139, pred[]{:T(512)S(6)} %compare.3, bf16[768,4096]{1,0:T(8,128)(2,1)} %get-tuple-element.149, s32[]{:T(128)S(6)} %select_n.25, bf16[768,3328]{1,0:T(8,128)(2,1)} %get-tuple-element.148), kind=kOutput, calls=%fused_computation.clone.1 | convolution fusion | flops 2658140160 | bytes 110478848 | tf_op jit(solution)/shard_map/while/body/eval_jaxpr/dot_general | solution.py:27
  436.4 36.3 %select_add_fusion.2 = f32[3328,4096]{1,0:T(8,128)} fusion(f32[3328,4096]{1,0:T(8,128)} %get-tuple-element.139, pred[]{:T(512)S(6)} %compare.3, bf16[768,4096]{1,0:T(8,128)(2,1)} %get-tuple-element.149, s32[]{:T(128)S(6)} %select_n.25, bf16[768,3328]{1,0:T(8,128)(2,1)} %get-tuple-element.148), kind=kOutput, calls=%fused_computation.clone.1 | convolution fusion | flops 2658140160 | bytes 110478848 | tf_op jit(solution)/shard_map/while/body/eval_jaxpr/dot_general | solution.py:27
  472.7 35.8 %broadcast_multiply_fusion = f32[3328,4096]{1,0:T(8,128)} fusion(f32[3328,4096]{1,0:T(8,128)} %get-tuple-element.81), kind=kLoop, calls=%fused_computation.4 | loop fusion | flops 13631488 | bytes 109051904 | tf_op jit(solution)/shard_map/div | solution.py:33
  508.4 2.9 convert_element_type.3
  (6 shorter events, 0.0 us)
Async XLA Ops:
  7.2 138.3 %copy-start.1 = (bf16[96,4096]{1,0:T(8,128)(2,1)S(1)}, bf16[96,4096]{1,0:T(8,128)(2,1)}, u32[]{:S(2)}) copy-start(bf16[96,4096]{1,0:T(8,128)(2,1)} %param.6) | copy-start | bytes 2359300
  7.2 183.1 %all-gather.2.cloned.1.call-start = ((), (), s32[]{:S(2)}) async-start(), calls=%async_computation.1 | async-start | bytes 6389760 | tf_op jit(solution)/shard_map/all_gather | solution.py:11
  7.2 23.2 %collective-permute-start = (bf16[96,4096]{1,0:T(8,128)(2,1)}, bf16[96,4096]{1,0:T(8,128)(2,1)S(1)}, u32[]{:S(2)}, u32[]{:S(2)}) collective-permute-start(bf16[96,4096]{1,0:T(8,128)(2,1)} %param.6), channel_id=1, source_target_pairs={{0,28},{4,0},{8,4},{12,8},{16,12},{20,16},{24,20},{28,24},{1,29},{... | collective-permute-start | bytes 2359304 | tf_op jit(solution)/shard_map/ppermute | solution.py:16
  30.4 21.0 %collective-permute-start.1 = (bf16[96,4096]{1,0:T(8,128)(2,1)S(1)}, bf16[96,4096]{1,0:T(8,128)(2,1)S(1)}, u32[]{:S(2)}, u32[]{:S(2)}) collective-permute-start(bf16[96,4096]{1,0:T(8,128)(2,1)S(1)} %collective-permute-done), channel_id=1, source_target_pairs={{0,28},{4,0},{8,4},{12,8},{16,12},{20,16},{24,20},{28,24},{1,29},{... | collective-permute-start | bytes 2359304 | tf_op jit(solution)/shard_map/ppermute | solution.py:16
  51.4 20.3 %collective-permute-start.2 = (bf16[96,4096]{1,0:T(8,128)(2,1)S(1)}, bf16[96,4096]{1,0:T(8,128)(2,1)S(1)}, u32[]{:S(2)}, u32[]{:S(2)}) collective-permute-start(bf16[96,4096]{1,0:T(8,128)(2,1)S(1)} %collective-permute-done.1), channel_id=1, source_target_pairs={{0,28},{4,0},{8,4},{12,8},{16,12},{20,16},{24,20},{28,24},{1,29},{... | collective-permute-start | bytes 2359304 | tf_op jit(solution)/shard_map/ppermute | solution.py:16
  71.7 19.4 %collective-permute-start.3 = (bf16[96,4096]{1,0:T(8,128)(2,1)S(1)}, bf16[96,4096]{1,0:T(8,128)(2,1)}, u32[]{:S(2)}, u32[]{:S(2)}) collective-permute-start(bf16[96,4096]{1,0:T(8,128)(2,1)S(1)} %collective-permute-done.2), channel_id=1, source_target_pairs={{0,28},{4,0},{8,4},{12,8},{16,12},{20,16},{24,20},{28,24},{1,29},{... | collective-permute-start | bytes 2359304 | tf_op jit(solution)/shard_map/ppermute | solution.py:16
  76.9 431.5 %reduce-scatter.2.cloned.1.call-start = ((), (), s32[]{:S(2)}) async-start(), calls=%async_computation.2 | async-start | bytes 12779520 | tf_op jit(solution)/shard_map/reduce_scatter | solution.py:34
  91.1 19.0 %collective-permute-start.4 = (bf16[96,4096]{1,0:T(8,128)(2,1)}, bf16[96,4096]{1,0:T(8,128)(2,1)S(1)}, u32[]{:S(2)}, u32[]{:S(2)}) collective-permute-start(bf16[96,4096]{1,0:T(8,128)(2,1)} %collective-permute-done.3), channel_id=1, source_target_pairs={{0,28},{4,0},{8,4},{12,8},{16,12},{20,16},{24,20},{28,24},{1,29},{... | collective-permute-start | bytes 2359304 | tf_op jit(solution)/shard_map/ppermute | solution.py:16
  110.1 17.6 %collective-permute-start.5 = (bf16[96,4096]{1,0:T(8,128)(2,1)S(1)}, bf16[96,4096]{1,0:T(8,128)(2,1)S(1)}, u32[]{:S(2)}, u32[]{:S(2)}) collective-permute-start(bf16[96,4096]{1,0:T(8,128)(2,1)S(1)} %collective-permute-done.4), channel_id=1, source_target_pairs={{0,28},{4,0},{8,4},{12,8},{16,12},{20,16},{24,20},{28,24},{1,29},{... | collective-permute-start | bytes 2359304 | tf_op jit(solution)/shard_map/ppermute | solution.py:16
  127.7 16.9 %collective-permute-start.6 = (bf16[96,4096]{1,0:T(8,128)(2,1)S(1)}, bf16[96,4096]{1,0:T(8,128)(2,1)S(1)}, u32[]{:S(2)}, u32[]{:S(2)}) collective-permute-start(bf16[96,4096]{1,0:T(8,128)(2,1)S(1)} %collective-permute-done.5), channel_id=1, source_target_pairs={{0,28},{4,0},{8,4},{12,8},{16,12},{20,16},{24,20},{28,24},{1,29},{... | collective-permute-start | bytes 2359304 | tf_op jit(solution)/shard_map/ppermute | solution.py:16
  159.0 2.6 copy-start
Sparse Core Ops, SparseCore 0:
  77.0 36.9 all-gather.1
  190.4 84.5 reduce-scatter.1
